TPU v7x, 32 devices: a whole 2x2x4 slice. The times are simulated.
32 devices in a mesh: samp: 8 (over y, x, core), sx: 2 (over z_hi), sy: 2 (over z_lo).
Axes of the slice: x: 2, y: 2, z: 4 (z_hi: 2, z_lo: 2; z = z_hi * 2 + z_lo), core: 2. Of those that a mesh axis runs over, the one named last changes fastest.
Arguments:
- volume: bfloat16 [8, 32, 4, 16, 128], P('samp', None, 'sx', 'sy'), may hold values from -6 to 6
- kernel: bfloat16 [64, 32, 3, 3, 3], replicated, may hold values from -0.21875 to 0.21875
- bias: float32 [64], replicated, may hold values from -4 to 4
- upstream: bfloat16 [8, 64, 4, 16, 128], P('samp', None, 'sx', 'sy'), may hold values from -6 to 6
Outputs:
- activated: bfloat16 [8, 64, 4, 16, 128], P('samp', None, 'sx', 'sy')
- input_grad: bfloat16 [8, 32, 4, 16, 128], P('samp', None, 'sx', 'sy')
- filter_grad: float32 [64, 32, 3, 3, 3], replicated
- bias_grad: float32 [64], replicated
All inputs are finite; a program needn't handle non-finite values.
Results may differ from a plain program's by a relative error of at most 0.0065.
Values may be sent and summed in bfloat16 or wider, within the bound.
A program may use at most 64 MiB of HBM per device.

v0:
```python
import jax
import jax.numpy as jnp
from jax import lax
from jax.sharding import PartitionSpec as P


def extended(shard, sides, width):
    for axis, dim in sides:
        size, length = (lax.axis_size(axis), shard.shape[dim])
        up = [(i, (i + 1) % size) for i in range(size - 1)]
        down = [(j, i) for i, j in up]
        last = lax.slice_in_dim(shard, length - width, length, axis=dim)
        initial = lax.slice_in_dim(shard, 0, width, axis=dim)
        before = lax.ppermute(last, axis, up)
        after = lax.ppermute(initial, axis, down)
        shard = jnp.concatenate([before, shard, after], axis=dim)
    return shard


def conv_forward(padded, kernel):
    return lax.conv_general_dilated(
        padded,
        kernel,
        (1, 1, 1),
        ((0, 0), (0, 0), (1, 1)),
        dimension_numbers=("NCDHW", "OIDHW", "NCDHW"),
        preferred_element_type=jnp.float32,
    )


def conv_backward(padded, kernel):
    flipped = kernel[:, :, ::-1, ::-1, ::-1]
    return lax.conv_general_dilated(
        padded,
        flipped,
        (1, 1, 1),
        ((0, 0), (0, 0), (1, 1)),
        dimension_numbers=("NCDHW", "IODHW", "NCDHW"),
        preferred_element_type=jnp.float32,
    )


def filter_terms(padded, delta):
    return lax.conv_general_dilated(
        padded,
        delta,
        (1, 1, 1),
        ((0, 0), (0, 0), (1, 1)),
        dimension_numbers=("CNDHW", "IODHW", "CNDHW"),
        preferred_element_type=jnp.float32,
    )


def slope_of(pre):
    return 0.3 + 0.7 * jax.nn.sigmoid(pre)


def per_device(volume, kernel, bias, upstream):
    samples, rows, cols, depth = (
        volume.shape[0],
        volume.shape[2],
        volume.shape[3],
        volume.shape[4],
    )
    bias_wide = bias[None, :, None, None, None]
    padded = extended(volume, (("sx", 2), ("sy", 3)), 1)
    pre = conv_forward(padded, kernel) + bias_wide
    delta = (upstream.astype(jnp.float32) * slope_of(pre)).astype(jnp.bfloat16)
    delta_pad = extended(delta, (("sx", 2), ("sy", 3)), 1)
    activated = (0.3 * pre + 0.7 * jax.nn.softplus(pre)).astype(jnp.bfloat16)
    input_grad = conv_backward(delta_pad, kernel).astype(jnp.bfloat16)
    wgrad = filter_terms(padded, delta)
    bgrad = jnp.sum(delta.astype(jnp.float32), axis=(0, 2, 3, 4))
    groups = lax.axis_size("sx") * lax.axis_size("sy")
    whole = lax.axis_size("samp") * samples * groups * rows * cols * depth
    norm = 1.0 / jnp.sqrt(jnp.float32(whole))
    wsum, bsum = lax.psum((wgrad, bgrad), ("samp", "sx", "sy"))
    return (activated, input_grad, wsum * norm, bsum * norm)


def solution(mesh):
    in_specs = (P("samp", None, "sx", "sy", None), P(), P(), P("samp", None, "sx", "sy", None))
    out_specs = (P("samp", None, "sx", "sy", None), P("samp", None, "sx", "sy", None), P(), P())
    return jax.shard_map(
        per_device, mesh=mesh, in_specs=in_specs, out_specs=out_specs, check_vma=False
    )
```

profile of v0, /device:TPU:8, one launch (start us, length us, event | category | flops | bytes accessed | tf_op | source)
XLA Modules:
  0.0 222.5 jit_solution(1578653945424406039)
XLA Ops:
  7.2 0.0 copy-start
  7.2 0.0 all-reduce.2.cloned.1.call-start
  7.2 0.9 fusion.47
  8.2 1.3 collective-permute-start.1
  9.5 5.4 %collective-permute-start = (bf16[1,32,1,8,128]{4,3,2,1,0:T(8,128)(2,1)S(1)}, bf16[1,32,1,8,128]{4,3,2,1,0:T(8,128)(2,1)S(1)}, u32[]{:S(2)}, u32[]{:S(2)}) collective-permute-start(bf16[1,32,1,8,128]{4,3,2,1,0:T(8,128)(2,1)S(1)} %get-tuple-element.26), channel_id=1, source_target_pairs={{0,2},{1,3},{4,6},{5,7},{8,10},{9,11},{12,14},{13,15},{16,18},{17,... | collective-permute-start | bytes 196616 | tf_op jit(solution)/shard_map/ppermute | solution.py:14
  14.9 0.3 collective-permute-done.1
  15.2 1.6 collective-permute-done
  16.8 1.0 pad_maximum_fusion.2
  17.8 0.0 copy-start.3
  17.8 1.2 copy.49
  19.0 1.3 fusion.44
  20.3 1.4 collective-permute-start.3
  21.7 1.3 collective-permute-start.2
  23.0 0.0 copy-done.3
  23.0 0.4 copy.57
  23.4 3.7 %collective-permute-done.3 = bf16[1,32,4,1,128]{1,0,4,3,2:T(2,128)(2,1)S(1)} collective-permute-done((bf16[1,32,4,1,128]{1,0,4,3,2:T(2,128)(2,1)}, bf16[1,32,4,1,128]{1,0,4,3,2:T(2,128)(2,1)S(1)}, u32[]{:S(2)}, u32[]{:S(2)}) %collective-permute-start.3) | collective-permute-done | bytes 32800 | tf_op jit(solution)/shard_map/ppermute | solution.py:15
  27.2 4.1 %collective-permute-done.2 = bf16[1,32,4,1,128]{1,0,4,3,2:T(2,128)(2,1)} collective-permute-done((bf16[1,32,4,1,128]{1,0,4,3,2:T(2,128)(2,1)}, bf16[1,32,4,1,128]{1,0,4,3,2:T(2,128)(2,1)}, u32[]{:S(2)}, u32[]{:S(2)}) %collective-permute-start.2) | collective-permute-done | bytes 32800 | tf_op jit(solution)/shard_map/ppermute | solution.py:14
  31.3 6.7 %pad_maximum_fusion = bf16[1,32,4,10,128]{1,0,4,3,2:T(2,128)(2,1)} fusion(bf16[1,32,4,1,128]{1,0,4,3,2:T(2,128)(2,1)S(1)} %collective-permute-done.3, bf16[1,32,4,8,128]{1,0,4,3,2:T(2,128)(2,1)S(1)} %copy.49, bf16[1,32,4,1,128]{1,0,4,3,2:T(2,128)(2,1)} %collective-permute-done.2), kind=kLoop, calls=%fused_computation.5 | loop fusion | flops 327680 | bytes 655360 | tf_op jit(solution)/shard_map/concatenate | solution.py:16
  38.1 4.7 %copy.52 = bf16[1,32,4,10,128]{4,1,3,2,0:T(8,128)(2,1)S(1)} copy(bf16[1,32,4,10,128]{1,0,4,3,2:T(2,128)(2,1)} %pad_maximum_fusion) | data formatting | bytes 655360 | tf_op jit(solution)/shard_map/concatenate | solution.py:16
  42.8 1.0 copy.69
  43.7 0.7 pad.clone
  44.4 0.0 copy-start.7
  44.4 0.0 copy-start.8
  44.5 0.2 copy.55
  44.7 0.0 copy-done
  44.7 0.4 copy-done.7
  45.1 0.0 copy-done.8
  45.1 3.4 %multiply_add_fusion = (f32[2,8,8,17,64]{4,2,3,1,0:T(8,128)S(1)}, bf16[2,8,8,17,64]{4,2,3,1,0:T(8,128)(2,1)}) fusion(f32[64]{0:T(128)S(1)} %copy-done.7, bf16[64,32,3,3,3]{0,1,4,3,2:T(8,128)(2,1)S(1)} %copy-done, bf16[32,4,10,1,7,2]{0,4,5,2,1,3:T(8,128)(2,1)S(1)} %slice.39, bf16[32,4,10,1,8,17]{0,4,5,2,1,3:T(8,128)(2,1)S(1)} %copy.55, ...), kind=kOutput, calls=%fused_computation.25 | convolution fusion | flops 244183040 | bytes 1330568 | tf_op jit(solution)/shard_map/conv_general_dilated | solution.py:21
  48.6 0.2 copy.58
  48.8 0.8 convert_reduce_fusion
  49.6 0.8 fusion.46
  50.4 0.1 copy-done.1
  50.5 15.8 %fusion.33 = f32[64,32,3,3,3]{0,1,4,3,2:T(8,128)} fusion(bf16[1,32,4,10,128]{1,0,4,3,2:T(2,128)(2,1)S(1)} %copy-done.1, bf16[1,64,2,8,128]{1,3,4,2,0:T(8,128)(2,1)S(1)} %get-tuple-element.17), kind=kOutput, calls=%fused_computation.31 | convolution fusion | flops 225312768 | bytes 811008 | tf_op jit(solution)/shard_map/conv_general_dilated | solution.py:44
  66.3 0.1 copy.56
  66.4 0.0 copy-start.6
  66.5 1.1 copy.67
  67.6 1.3 collective-permute-start.5
  68.9 0.0 copy-done.4
  68.9 5.5 %collective-permute-start.4 = (bf16[1,64,1,8,128]{1,3,4,2,0:T(8,128)(2,1)S(1)}, bf16[1,64,1,8,128]{1,3,4,2,0:T(8,128)(2,1)S(1)}, u32[]{:S(2)}, u32[]{:S(2)}) collective-permute-start(bf16[1,64,1,8,128]{1,3,4,2,0:T(8,128)(2,1)S(1)} %copy-done.4), channel_id=1, source_target_pairs={{0,2},{1,3},{4,6},{5,7},{8,10},{9,11},{12,14},{13,15},{16,18},{17,... | collective-permute-start | bytes 393224 | tf_op jit(solution)/shard_map/ppermute | solution.py:14
  74.4 0.0 all-reduce.2.cloned.1.call-update
  74.4 38.9 %psum.15 = f32[64]{0:T(128)S(1)} all-reduce(f32[64]{0:T(128)S(1)} %copy-done.6), channel_id=1, replica_groups=mesh['samp'=8,'sx'=2,'sy'=2] {'samp','sx','sy'}, use_global_device_ids=true, to_apply=%region_2.3 | all-reduce | flops 64 | bytes 512 | tf_op jit(solution)/shard_map/psum | solution.py:77
  113.4 0.5 broadcast_multiply_fusion.1
  113.9 0.0 collective-permute-done.5
  113.9 0.0 collective-permute-done.4
  113.9 0.2 pad_maximum_fusion.1
  114.1 0.3 fusion.45
  114.5 4.0 %collective-permute-start.7 = (bf16[1,64,4,1,128]{1,3,4,2,0:T(2,128)(2,1)S(1)}, bf16[1,64,4,1,128]{1,3,4,2,0:T(2,128)(2,1)S(1)}, u32[]{:S(2)}, u32[]{:S(2)}) collective-permute-start(bf16[1,64,4,1,128]{1,3,4,2,0:T(2,128)(2,1)S(1)} %get-tuple-element.23), channel_id=1, source_target_pairs={{1,0},{3,2},{5,4},{7,6},{9,8},{11,10},{13,12},{15,14},{17,16},{19,... | collective-permute-start | bytes 196616 | tf_op jit(solution)/shard_map/ppermute | solution.py:15
  118.5 1.3 collective-permute-start.6
  119.8 84.6 %all-reduce.2.cloned.1.call-done = f32[64,32,3,3,3]{0,1,4,3,2:T(8,128)} async-done(((f32[64,32,3,3,3]{0,1,4,3,2:T(8,128)}), f32[64,32,3,3,3]{0,1,4,3,2:T(8,128)}) %all-reduce.2.cloned.1.call-update) | async-done | bytes 221200 | tf_op jit(solution)/shard_map/psum | solution.py:77
  204.4 1.8 broadcast_multiply_fusion
  206.2 0.6 copy.60
  206.8 0.0 collective-permute-done.7
  206.8 0.1 copy.61
  207.0 0.0 collective-permute-done.6
  207.0 0.1 copy.59
  207.1 0.1 maximum_bitcast_fusion
  207.2 1.9 copy.70
  209.1 0.7 pad.2.clone
  209.8 0.0 copy-start.9
  209.8 0.2 copy.64
  210.0 0.4 copy-done.9
  210.4 4.0 %fusion.25 = bf16[2,8,8,17,32]{4,2,3,1,0:T(8,128)(2,1)S(1)} fusion(bf16[64,32,3,3,3]{0,1,4,3,2:T(8,128)(2,1)S(1)} %copy-done, bf16[64,4,10,1,7,2]{0,4,5,2,1,3:T(8,128)(2,1)S(1)} %slice.46, bf16[64,4,10,1,8,17]{0,4,5,2,1,3:T(8,128)(2,1)S(1)} %copy.64, pred[8,17]{0,1:T(8,128)(4,1)S(1)} %copy-done.9), kind=kOutput, calls=%fused_computation.21 | convolution fusion | flops 243122176 | bytes 1017992 | tf_op jit(solution)/shard_map/conv_general_dilated | solution.py:33
  214.5 0.1 copy.65
  214.6 1.0 copy.68
  (11 shorter events, 0.2 us)
Async XLA Ops:
  7.2 37.5 %copy-start = (bf16[64,32,3,3,3]{0,1,4,3,2:T(8,128)(2,1)S(1)}, bf16[64,32,3,3,3]{0,1,4,3,2:T(8,128)(2,1)}, u32[]{:S(2)}) copy-start(bf16[64,32,3,3,3]{0,1,4,3,2:T(8,128)(2,1)} %param.5) | copy-start | bytes 331780
  7.2 197.2 %all-reduce.2.cloned.1.call-start = ((), (), s32[]{:S(2)}) async-start(), calls=%async_computation | async-start | bytes 884736 | tf_op jit(solution)/shard_map/psum | solution.py:77
  8.2 7.1 %collective-permute-start.1 = (bf16[1,32,1,8,128]{4,3,2,1,0:T(8,128)(2,1)S(1)}, bf16[1,32,1,8,128]{4,3,2,1,0:T(8,128)(2,1)S(1)}, u32[]{:S(2)}, u32[]{:S(2)}) collective-permute-start(bf16[1,32,1,8,128]{4,3,2,1,0:T(8,128)(2,1)S(1)} %get-tuple-element.27), channel_id=1, source_target_pairs={{2,0},{3,1},{6,4},{7,5},{10,8},{11,9},{14,12},{15,13},{18,16},{19,... | collective-permute-start | bytes 196616 | tf_op jit(solution)/shard_map/ppermute | solution.py:15
  9.5 7.3 %collective-permute-start = (bf16[1,32,1,8,128]{4,3,2,1,0:T(8,128)(2,1)S(1)}, bf16[1,32,1,8,128]{4,3,2,1,0:T(8,128)(2,1)S(1)}, u32[]{:S(2)}, u32[]{:S(2)}) collective-permute-start(bf16[1,32,1,8,128]{4,3,2,1,0:T(8,128)(2,1)S(1)} %get-tuple-element.26), channel_id=1, source_target_pairs={{0,2},{1,3},{4,6},{5,7},{8,10},{9,11},{12,14},{13,15},{16,18},{17,... | collective-permute-start | bytes 196616 | tf_op jit(solution)/shard_map/ppermute | solution.py:14
  17.8 5.3 %copy-start.3 = (bf16[1,64,2,8,128]{4,3,2,1,0:T(8,128)(2,1)S(1)}, bf16[1,64,2,8,128]{4,3,2,1,0:T(8,128)(2,1)}, u32[]{:S(2)}) copy-start(bf16[1,64,2,8,128]{4,3,2,1,0:T(8,128)(2,1)} %param.7) | copy-start | bytes 786436
  20.3 6.9 %collective-permute-start.3 = (bf16[1,32,4,1,128]{1,0,4,3,2:T(2,128)(2,1)}, bf16[1,32,4,1,128]{1,0,4,3,2:T(2,128)(2,1)S(1)}, u32[]{:S(2)}, u32[]{:S(2)}) collective-permute-start(bf16[1,32,4,1,128]{1,0,4,3,2:T(2,128)(2,1)} %get-tuple-element.19), channel_id=1, source_target_pairs={{1,0},{3,2},{5,4},{7,6},{9,8},{11,10},{13,12},{15,14},{17,16},{19,... | collective-permute-start | bytes 98312 | tf_op jit(solution)/shard_map/ppermute | solution.py:15
  21.7 9.6 %collective-permute-start.2 = (bf16[1,32,4,1,128]{1,0,4,3,2:T(2,128)(2,1)}, bf16[1,32,4,1,128]{1,0,4,3,2:T(2,128)(2,1)}, u32[]{:S(2)}, u32[]{:S(2)}) collective-permute-start(bf16[1,32,4,1,128]{1,0,4,3,2:T(2,128)(2,1)} %get-tuple-element.18), channel_id=1, source_target_pairs={{0,1},{2,3},{4,5},{6,7},{8,9},{10,11},{12,13},{14,15},{16,17},{18,... | collective-permute-start | bytes 98312 | tf_op jit(solution)/shard_map/ppermute | solution.py:14
  44.4 0.7 copy-start.7
  44.4 0.7 copy-start.8
  48.8 1.7 copy-start.1
  50.5 15.8 %copy-start.2 = (bf16[2,8,8,17,64]{4,2,3,1,0:T(8,128)(2,1)S(1)}, bf16[2,8,8,17,64]{4,2,3,1,0:T(8,128)(2,1)}, u32[]{:S(2)}) copy-start(bf16[2,8,8,17,64]{4,2,3,1,0:T(8,128)(2,1)} %get-tuple-element.21) | copy-start | bytes 835588
  66.3 1.3 copy-start.5
  66.3 2.6 %copy-start.4 = (bf16[1,64,1,8,128]{1,3,4,2,0:T(8,128)(2,1)S(1)}, bf16[1,64,1,8,128]{1,3,4,2,0:T(8,128)(2,1)}, u32[]{:S(2)}) copy-start(bf16[1,64,1,8,128]{1,3,4,2,0:T(8,128)(2,1)} %get-tuple-element.24) | copy-start | bytes 393220
  66.4 8.0 %copy-start.6 = (f32[64]{0:T(128)S(1)}, f32[64]{0:T(128)}, u32[]{:S(2)}) copy-start(f32[64]{0:T(128)} %get-tuple-element.16) | copy-start | bytes 772
  67.6 46.3 %collective-permute-start.5 = (bf16[1,64,1,8,128]{1,3,4,2,0:T(8,128)(2,1)S(1)}, bf16[1,64,1,8,128]{1,3,4,2,0:T(8,128)(2,1)S(1)}, u32[]{:S(2)}, u32[]{:S(2)}) collective-permute-start(bf16[1,64,1,8,128]{1,3,4,2,0:T(8,128)(2,1)S(1)} %copy-done.5), channel_id=1, source_target_pairs={{2,0},{3,1},{6,4},{7,5},{10,8},{11,9},{14,12},{15,13},{18,16},{19,... | collective-permute-start | bytes 393224 | tf_op jit(solution)/shard_map/ppermute | solution.py:15
  68.9 45.0 %collective-permute-start.4 = (bf16[1,64,1,8,128]{1,3,4,2,0:T(8,128)(2,1)S(1)}, bf16[1,64,1,8,128]{1,3,4,2,0:T(8,128)(2,1)S(1)}, u32[]{:S(2)}, u32[]{:S(2)}) collective-permute-start(bf16[1,64,1,8,128]{1,3,4,2,0:T(8,128)(2,1)S(1)} %copy-done.4), channel_id=1, source_target_pairs={{0,2},{1,3},{4,6},{5,7},{8,10},{9,11},{12,14},{13,15},{16,18},{17,... | collective-permute-start | bytes 393224 | tf_op jit(solution)/shard_map/ppermute | solution.py:14
  114.5 92.3 %collective-permute-start.7 = (bf16[1,64,4,1,128]{1,3,4,2,0:T(2,128)(2,1)S(1)}, bf16[1,64,4,1,128]{1,3,4,2,0:T(2,128)(2,1)S(1)}, u32[]{:S(2)}, u32[]{:S(2)}) collective-permute-start(bf16[1,64,4,1,128]{1,3,4,2,0:T(2,128)(2,1)S(1)} %get-tuple-element.23), channel_id=1, source_target_pairs={{1,0},{3,2},{5,4},{7,6},{9,8},{11,10},{13,12},{15,14},{17,16},{19,... | collective-permute-start | bytes 196616 | tf_op jit(solution)/shard_map/ppermute | solution.py:15
  118.5 88.5 %collective-permute-start.6 = (bf16[1,64,4,1,128]{1,3,4,2,0:T(2,128)(2,1)S(1)}, bf16[1,64,4,1,128]{1,3,4,2,0:T(2,128)(2,1)S(1)}, u32[]{:S(2)}, u32[]{:S(2)}) collective-permute-start(bf16[1,64,4,1,128]{1,3,4,2,0:T(2,128)(2,1)S(1)} %get-tuple-element.22), channel_id=1, source_target_pairs={{0,1},{2,3},{4,5},{6,7},{8,9},{10,11},{12,13},{14,15},{16,17},{18,... | collective-permute-start | bytes 196616 | tf_op jit(solution)/shard_map/ppermute | solution.py:14
  209.8 0.7 copy-start.9
Sparse Core Ops, SparseCore 0:
  74.5 129.7 all-reduce.1
where the time goes:
time: 223 us; the launch traced here: 222 us
  waiting for transfers between devices  94.3 us (42%)
  blocking collectives  38.9 us (17%)
  matrix products  23.3 us (10%)
  starting transfers between devices  21.5 us (10%)
  local copies, waits for them, and re-layouts  18.9 us (8%)
  between operations  14.4 us (6%)
  other arithmetic  11.2 us (5%)
    psum x1, waiting for transfers between devices, per_device(): wsum, bsum = lax.psum((wgrad, bgrad), ('samp', 'sx', 'sy'))  84.6 us
    psum x1, blocking collectives, per_device(): wsum, bsum = lax.psum((wgrad, bgrad), ('samp', 'sx', 'sy'))  38.9 us
    conv_general_dilated x1, matrix products, filter_terms(): lax.conv_general_dilated(padded, delta, (1, 1, 1), ((0, 0), (0, 0), (1, 1...  15.8 us
    ppermute x4, starting transfers between devices, extended(): before = lax.ppermute(last, axis, up)  13.5 us
    concatenate x4, other arithmetic, extended(): shard = jnp.concatenate([before, shard, after], axis=dim)  8.04 us
    ppermute x4, starting transfers between devices, extended(): after = lax.ppermute(initial, axis, down)  7.99 us
    concatenate x5, local copies, waits for them, and re-layouts, extended(): shard = jnp.concatenate([before, shard, after], axis=dim)  7.9 us
    unnamed x25, local copies, waits for them, and re-layouts  6.4 us
  transfers between devices with their start and end apart: 9, of which 5 were waited for; matrix products, arithmetic and copies ran while one was open for 2% of the time, Pallas kernels for 0%

commit v1 on v0

--- a/solution.py
+++ b/solution.py
@@ -74,7 +74,7 @@
     groups = lax.axis_size("sx") * lax.axis_size("sy")
     whole = lax.axis_size("samp") * samples * groups * rows * cols * depth
     norm = 1.0 / jnp.sqrt(jnp.float32(whole))
-    wsum, bsum = lax.psum((wgrad, bgrad), ("samp", "sx", "sy"))
+    wsum, bsum = lax.psum(lax.psum((wgrad, bgrad), ("sx", "sy")), "samp")
     return (activated, input_grad, wsum * norm, bsum * norm)
 
 

time: 223 us -> 189 us (0.85)
  waiting for transfers between devices: 94.3 us -> 76.6 us
  blocking collectives: 38.9 us -> 23.6 us
  starting transfers between devices: 21.5 us -> 18.9 us
    psum x1 -> x2, waiting for transfers between devices: 84.6 us -> 54.8 us  [per_device(): wsum, bsum = lax.psum(lax.psum((wgrad, bgrad), ('sx', 'sy')), 'samp')]
    psum x1 -> x2, blocking collectives: 38.9 us -> 23.6 us  [per_device(): wsum, bsum = lax.psum(lax.psum((wgrad, bgrad), ('sx', 'sy')), 'samp')]
    ppermute x4, waiting for transfers between devices: 4.05 us -> 14.3 us  [extended(): after = lax.ppermute(initial, axis, down)]
    ppermute x4, starting transfers between devices: 7.99 us -> 5.3 us  [extended(): after = lax.ppermute(initial, axis, down)]
  transfers between devices with their start and end apart: 9 -> 10, of which waited for: 5 -> 7; matrix products, arithmetic and copies ran while one was open for 2% -> 6% of each run, Pallas kernels for 0% -> 0%
where the time goes in v1:
time: 189 us; the launch traced here: 187 us
  waiting for transfers between devices  76.6 us (41%)
  blocking collectives  23.6 us (12%)
  matrix products  23.3 us (12%)
  local copies, waits for them, and re-layouts  18.9 us (10%)
  starting transfers between devices  18.9 us (10%)
  between operations  14.4 us (8%)
  other arithmetic  11.1 us (6%)
    psum x2, waiting for transfers between devices, per_device(): wsum, bsum = lax.psum(lax.psum((wgrad, bgrad), ('sx', 'sy')), 'samp')  54.8 us
    psum x2, blocking collectives, per_device(): wsum, bsum = lax.psum(lax.psum((wgrad, bgrad), ('sx', 'sy')), 'samp')  23.6 us
    conv_general_dilated x1, matrix products, filter_terms(): lax.conv_general_dilated(padded, delta, (1, 1, 1), ((0, 0), (0, 0), (1, 1...  15.8 us
    ppermute x4, waiting for transfers between devices, extended(): after = lax.ppermute(initial, axis, down)  14.3 us
    ppermute x4, starting transfers between devices, extended(): before = lax.ppermute(last, axis, up)  13.5 us
    concatenate x4, other arithmetic, extended(): shard = jnp.concatenate([before, shard, after], axis=dim)  8.01 us
    concatenate x5, local copies, waits for them, and re-layouts, extended(): shard = jnp.concatenate([before, shard, after], axis=dim)  7.9 us
    ppermute x4, waiting for transfers between devices, extended(): before = lax.ppermute(last, axis, up)  7.45 us
  transfers between devices with their start and end apart: 10, of which 7 were waited for; matrix products, arithmetic and copies ran while one was open for 6% of the time, Pallas kernels for 0%

profile of v1, /device:TPU:8, one launch (start us, length us, event | category | flops | bytes accessed | tf_op | source)
XLA Modules:
  0.0 186.7 jit_solution(8286435160365967825)
XLA Ops:
  7.2 0.0 copy-start
  7.2 0.0 all-reduce.3.cloned.1.call-start
  7.2 0.9 fusion.47
  8.2 1.3 collective-permute-start.1
  9.5 5.4 %collective-permute-start = (bf16[1,32,1,8,128]{4,3,2,1,0:T(8,128)(2,1)S(1)}, bf16[1,32,1,8,128]{4,3,2,1,0:T(8,128)(2,1)S(1)}, u32[]{:S(2)}, u32[]{:S(2)}) collective-permute-start(bf16[1,32,1,8,128]{4,3,2,1,0:T(8,128)(2,1)S(1)} %get-tuple-element.26), channel_id=1, source_target_pairs={{0,2},{1,3},{4,6},{5,7},{8,10},{9,11},{12,14},{13,15},{16,18},{17,... | collective-permute-start | bytes 196616 | tf_op jit(solution)/shard_map/ppermute | solution.py:14
  14.9 0.3 collective-permute-done.1
  15.2 1.6 collective-permute-done
  16.8 1.0 pad_maximum_fusion.2
  17.8 0.0 copy-start.3
  17.8 1.2 copy.49
  19.0 1.3 fusion.44
  20.3 1.4 collective-permute-start.3
  21.7 1.3 collective-permute-start.2
  23.0 0.4 copy.57
  23.4 3.7 %collective-permute-done.3 = bf16[1,32,4,1,128]{1,0,4,3,2:T(2,128)(2,1)S(1)} collective-permute-done((bf16[1,32,4,1,128]{1,0,4,3,2:T(2,128)(2,1)}, bf16[1,32,4,1,128]{1,0,4,3,2:T(2,128)(2,1)S(1)}, u32[]{:S(2)}, u32[]{:S(2)}) %collective-permute-start.3) | collective-permute-done | bytes 32800 | tf_op jit(solution)/shard_map/ppermute | solution.py:15
  27.2 4.1 %collective-permute-done.2 = bf16[1,32,4,1,128]{1,0,4,3,2:T(2,128)(2,1)} collective-permute-done((bf16[1,32,4,1,128]{1,0,4,3,2:T(2,128)(2,1)}, bf16[1,32,4,1,128]{1,0,4,3,2:T(2,128)(2,1)}, u32[]{:S(2)}, u32[]{:S(2)}) %collective-permute-start.2) | collective-permute-done | bytes 32800 | tf_op jit(solution)/shard_map/ppermute | solution.py:14
  31.3 6.7 %pad_maximum_fusion = bf16[1,32,4,10,128]{1,0,4,3,2:T(2,128)(2,1)} fusion(bf16[1,32,4,1,128]{1,0,4,3,2:T(2,128)(2,1)S(1)} %collective-permute-done.3, bf16[1,32,4,8,128]{1,0,4,3,2:T(2,128)(2,1)S(1)} %copy.49, bf16[1,32,4,1,128]{1,0,4,3,2:T(2,128)(2,1)} %collective-permute-done.2), kind=kLoop, calls=%fused_computation.5 | loop fusion | flops 327680 | bytes 655360 | tf_op jit(solution)/shard_map/concatenate | solution.py:16
  38.0 4.7 %copy.52 = bf16[1,32,4,10,128]{4,1,3,2,0:T(8,128)(2,1)S(1)} copy(bf16[1,32,4,10,128]{1,0,4,3,2:T(2,128)(2,1)} %pad_maximum_fusion) | data formatting | bytes 655360 | tf_op jit(solution)/shard_map/concatenate | solution.py:16
  42.7 1.0 copy.69
  43.7 0.7 pad.clone
  44.4 0.0 copy-start.7
  44.4 0.0 copy-start.8
  44.4 0.2 copy.55
  44.7 0.4 copy-done.7
  45.1 0.0 copy-done.8
  45.1 3.4 %multiply_add_fusion = (f32[2,8,8,17,64]{4,2,3,1,0:T(8,128)S(1)}, bf16[2,8,8,17,64]{4,2,3,1,0:T(8,128)(2,1)}) fusion(f32[64]{0:T(128)S(1)} %copy-done.7, bf16[64,32,3,3,3]{0,1,4,3,2:T(8,128)(2,1)S(1)} %copy-done, bf16[32,4,10,1,7,2]{0,4,5,2,1,3:T(8,128)(2,1)S(1)} %slice.39, bf16[32,4,10,1,8,17]{0,4,5,2,1,3:T(8,128)(2,1)S(1)} %copy.55, ...), kind=kOutput, calls=%fused_computation.25 | convolution fusion | flops 244183040 | bytes 1330568 | tf_op jit(solution)/shard_map/conv_general_dilated | solution.py:21
  48.5 0.2 copy.58
  48.8 0.8 convert_reduce_fusion
  49.6 0.8 fusion.46
  50.4 0.1 copy-done.1
  50.5 15.8 %fusion.33 = f32[64,32,3,3,3]{0,1,4,3,2:T(8,128)} fusion(bf16[1,32,4,10,128]{1,0,4,3,2:T(2,128)(2,1)S(1)} %copy-done.1, bf16[1,64,2,8,128]{1,3,4,2,0:T(8,128)(2,1)S(1)} %get-tuple-element.17), kind=kOutput, calls=%fused_computation.31 | convolution fusion | flops 225312768 | bytes 811008 | tf_op jit(solution)/shard_map/conv_general_dilated | solution.py:44
  66.3 0.1 copy.56
  66.4 0.0 copy-start.6
  66.4 1.3 collective-permute-start.5
  67.7 5.5 %collective-permute-start.4 = (bf16[1,64,1,8,128]{1,3,4,2,0:T(8,128)(2,1)S(1)}, bf16[1,64,1,8,128]{1,3,4,2,0:T(8,128)(2,1)S(1)}, u32[]{:S(2)}, u32[]{:S(2)}) collective-permute-start(bf16[1,64,1,8,128]{1,3,4,2,0:T(8,128)(2,1)S(1)} %copy-done.4), channel_id=1, source_target_pairs={{0,2},{1,3},{4,6},{5,7},{8,10},{9,11},{12,14},{13,15},{16,18},{17,... | collective-permute-start | bytes 393224 | tf_op jit(solution)/shard_map/ppermute | solution.py:14
  73.2 1.1 copy.67
  74.4 0.0 all-reduce.3.cloned.1.call-update
  74.4 0.0 all-reduce.5.cloned.1.call-start
  74.5 11.8 %psum.30 = f32[64]{0:T(128)S(1)} all-reduce(f32[64]{0:T(128)S(1)} %copy-done.6), channel_id=1, replica_groups=mesh['samp'=8,'sx'=2,'sy'=2] {'sx','sy'}, use_global_device_ids=true, to_apply=%region_3.4 | all-reduce | flops 64 | bytes 512 | tf_op jit(solution)/shard_map/psum | solution.py:77
  86.2 11.8 %psum.31 = f32[64]{0:T(128)S(1)} all-reduce(f32[64]{0:T(128)S(1)} %psum.30), channel_id=1, replica_groups=mesh['samp'=8,'sx'=2,'sy'=2] {'samp'}, use_global_device_ids=true, to_apply=%region_4.5 | all-reduce | flops 64 | bytes 512 | tf_op jit(solution)/shard_map/psum | solution.py:77
  98.0 0.0 collective-permute-done.5
  98.0 0.2 pad_maximum_fusion.1
  98.3 0.3 fusion.45
  98.6 1.3 collective-permute-start.7
  100.0 1.3 collective-permute-start.6
  101.3 0.5 broadcast_multiply_fusion.1
  101.8 0.6 copy.60
  102.4 10.2 %collective-permute-done.7 = bf16[1,64,4,1,128]{1,3,4,2,0:T(2,128)(2,1)S(1)} collective-permute-done((bf16[1,64,4,1,128]{1,3,4,2,0:T(2,128)(2,1)S(1)}, bf16[1,64,4,1,128]{1,3,4,2,0:T(2,128)(2,1)S(1)}, u32[]{:S(2)}, u32[]{:S(2)}) %collective-permute-start.7) | collective-permute-done | bytes 65568 | tf_op jit(solution)/shard_map/ppermute | solution.py:15
  112.6 0.1 copy.61
  112.8 1.7 collective-permute-done.6
  114.5 0.1 copy.59
  114.6 0.1 maximum_bitcast_fusion
  114.7 1.9 copy.70
  116.6 0.7 pad.2.clone
  117.3 0.0 copy-start.9
  117.3 0.2 copy.64
  117.5 0.4 copy-done.9
  118.0 4.0 %fusion.25 = bf16[2,8,8,17,32]{4,2,3,1,0:T(8,128)(2,1)S(1)} fusion(bf16[64,32,3,3,3]{0,1,4,3,2:T(8,128)(2,1)S(1)} %copy-done, bf16[64,4,10,1,7,2]{0,4,5,2,1,3:T(8,128)(2,1)S(1)} %slice.46, bf16[64,4,10,1,8,17]{0,4,5,2,1,3:T(8,128)(2,1)S(1)} %copy.64, pred[8,17]{0,1:T(8,128)(4,1)S(1)} %copy-done.9), kind=kOutput, calls=%fused_computation.21 | convolution fusion | flops 243122176 | bytes 1017992 | tf_op jit(solution)/shard_map/conv_general_dilated | solution.py:33
  122.0 0.1 copy.65
  122.1 0.0 all-reduce.3.cloned.1.call-done
  122.1 0.0 all-reduce.5.cloned.1.call-update
  122.2 1.0 copy.68
  123.2 54.8 %all-reduce.5.cloned.1.call-done = f32[64,32,3,3,3]{0,1,4,3,2:T(8,128)} async-done(((f32[64,32,3,3,3]{0,1,4,3,2:T(8,128)}), f32[64,32,3,3,3]{0,1,4,3,2:T(8,128)}) %all-reduce.5.cloned.1.call-update) | async-done | bytes 221200 | tf_op jit(solution)/shard_map/psum | solution.py:77
  178.0 1.8 broadcast_multiply_fusion
  (15 shorter events, 0.2 us)
Async XLA Ops:
  7.2 37.5 %copy-start = (bf16[64,32,3,3,3]{0,1,4,3,2:T(8,128)(2,1)S(1)}, bf16[64,32,3,3,3]{0,1,4,3,2:T(8,128)(2,1)}, u32[]{:S(2)}) copy-start(bf16[64,32,3,3,3]{0,1,4,3,2:T(8,128)(2,1)} %param.5) | copy-start | bytes 331780
  7.2 114.9 %all-reduce.3.cloned.1.call-start = ((), (), s32[]{:S(2)}) async-start(), calls=%async_computation | async-start | bytes 884736 | tf_op jit(solution)/shard_map/psum | solution.py:77
  8.2 7.1 %collective-permute-start.1 = (bf16[1,32,1,8,128]{4,3,2,1,0:T(8,128)(2,1)S(1)}, bf16[1,32,1,8,128]{4,3,2,1,0:T(8,128)(2,1)S(1)}, u32[]{:S(2)}, u32[]{:S(2)}) collective-permute-start(bf16[1,32,1,8,128]{4,3,2,1,0:T(8,128)(2,1)S(1)} %get-tuple-element.27), channel_id=1, source_target_pairs={{2,0},{3,1},{6,4},{7,5},{10,8},{11,9},{14,12},{15,13},{18,16},{19,... | collective-permute-start | bytes 196616 | tf_op jit(solution)/shard_map/ppermute | solution.py:15
  9.5 7.3 %collective-permute-start = (bf16[1,32,1,8,128]{4,3,2,1,0:T(8,128)(2,1)S(1)}, bf16[1,32,1,8,128]{4,3,2,1,0:T(8,128)(2,1)S(1)}, u32[]{:S(2)}, u32[]{:S(2)}) collective-permute-start(bf16[1,32,1,8,128]{4,3,2,1,0:T(8,128)(2,1)S(1)} %get-tuple-element.26), channel_id=1, source_target_pairs={{0,2},{1,3},{4,6},{5,7},{8,10},{9,11},{12,14},{13,15},{16,18},{17,... | collective-permute-start | bytes 196616 | tf_op jit(solution)/shard_map/ppermute | solution.py:14
  17.8 5.3 %copy-start.3 = (bf16[1,64,2,8,128]{4,3,2,1,0:T(8,128)(2,1)S(1)}, bf16[1,64,2,8,128]{4,3,2,1,0:T(8,128)(2,1)}, u32[]{:S(2)}) copy-start(bf16[1,64,2,8,128]{4,3,2,1,0:T(8,128)(2,1)} %param.7) | copy-start | bytes 786436
  20.3 6.9 %collective-permute-start.3 = (bf16[1,32,4,1,128]{1,0,4,3,2:T(2,128)(2,1)}, bf16[1,32,4,1,128]{1,0,4,3,2:T(2,128)(2,1)S(1)}, u32[]{:S(2)}, u32[]{:S(2)}) collective-permute-start(bf16[1,32,4,1,128]{1,0,4,3,2:T(2,128)(2,1)} %get-tuple-element.19), channel_id=1, source_target_pairs={{1,0},{3,2},{5,4},{7,6},{9,8},{11,10},{13,12},{15,14},{17,16},{19,... | collective-permute-start | bytes 98312 | tf_op jit(solution)/shard_map/ppermute | solution.py:15
  21.7 9.6 %collective-permute-start.2 = (bf16[1,32,4,1,128]{1,0,4,3,2:T(2,128)(2,1)}, bf16[1,32,4,1,128]{1,0,4,3,2:T(2,128)(2,1)}, u32[]{:S(2)}, u32[]{:S(2)}) collective-permute-start(bf16[1,32,4,1,128]{1,0,4,3,2:T(2,128)(2,1)} %get-tuple-element.18), channel_id=1, source_target_pairs={{0,1},{2,3},{4,5},{6,7},{8,9},{10,11},{12,13},{14,15},{16,17},{18,... | collective-permute-start | bytes 98312 | tf_op jit(solution)/shard_map/ppermute | solution.py:14
  44.4 0.7 copy-start.7
  44.4 0.7 copy-start.8
  48.7 1.7 copy-start.1
  50.5 15.8 %copy-start.2 = (bf16[2,8,8,17,64]{4,2,3,1,0:T(8,128)(2,1)S(1)}, bf16[2,8,8,17,64]{4,2,3,1,0:T(8,128)(2,1)}, u32[]{:S(2)}) copy-start(bf16[2,8,8,17,64]{4,2,3,1,0:T(8,128)(2,1)} %get-tuple-element.21) | copy-start | bytes 835588
  50.5 15.9 %copy-start.5 = (bf16[1,64,1,8,128]{1,3,4,2,0:T(8,128)(2,1)S(1)}, bf16[1,64,1,8,128]{1,3,4,2,0:T(8,128)(2,1)}, u32[]{:S(2)}) copy-start(bf16[1,64,1,8,128]{1,3,4,2,0:T(8,128)(2,1)} %get-tuple-element.25) | copy-start | bytes 393220
  50.5 17.2 %copy-start.4 = (bf16[1,64,1,8,128]{1,3,4,2,0:T(8,128)(2,1)S(1)}, bf16[1,64,1,8,128]{1,3,4,2,0:T(8,128)(2,1)}, u32[]{:S(2)}) copy-start(bf16[1,64,1,8,128]{1,3,4,2,0:T(8,128)(2,1)} %get-tuple-element.24) | copy-start | bytes 393220
  66.4 8.1 %copy-start.6 = (f32[64]{0:T(128)S(1)}, f32[64]{0:T(128)}, u32[]{:S(2)}) copy-start(f32[64]{0:T(128)} %get-tuple-element.16) | copy-start | bytes 772
  66.4 31.6 %collective-permute-start.5 = (bf16[1,64,1,8,128]{1,3,4,2,0:T(8,128)(2,1)S(1)}, bf16[1,64,1,8,128]{1,3,4,2,0:T(8,128)(2,1)S(1)}, u32[]{:S(2)}, u32[]{:S(2)}) collective-permute-start(bf16[1,64,1,8,128]{1,3,4,2,0:T(8,128)(2,1)S(1)} %copy-done.5), channel_id=1, source_target_pairs={{2,0},{3,1},{6,4},{7,5},{10,8},{11,9},{14,12},{15,13},{18,16},{19,... | collective-permute-start | bytes 393224 | tf_op jit(solution)/shard_map/ppermute | solution.py:15
  67.7 30.3 %collective-permute-start.4 = (bf16[1,64,1,8,128]{1,3,4,2,0:T(8,128)(2,1)S(1)}, bf16[1,64,1,8,128]{1,3,4,2,0:T(8,128)(2,1)S(1)}, u32[]{:S(2)}, u32[]{:S(2)}) collective-permute-start(bf16[1,64,1,8,128]{1,3,4,2,0:T(8,128)(2,1)S(1)} %copy-done.4), channel_id=1, source_target_pairs={{0,2},{1,3},{4,6},{5,7},{8,10},{9,11},{12,14},{13,15},{16,18},{17,... | collective-permute-start | bytes 393224 | tf_op jit(solution)/shard_map/ppermute | solution.py:14
  74.4 103.6 %all-reduce.5.cloned.1.call-start = ((), (), s32[]{:S(2)}) async-start(), calls=%async_computation.1 | async-start | bytes 884736 | tf_op jit(solution)/shard_map/psum | solution.py:77
  98.6 14.0 %collective-permute-start.7 = (bf16[1,64,4,1,128]{1,3,4,2,0:T(2,128)(2,1)S(1)}, bf16[1,64,4,1,128]{1,3,4,2,0:T(2,128)(2,1)S(1)}, u32[]{:S(2)}, u32[]{:S(2)}) collective-permute-start(bf16[1,64,4,1,128]{1,3,4,2,0:T(2,128)(2,1)S(1)} %get-tuple-element.23), channel_id=1, source_target_pairs={{1,0},{3,2},{5,4},{7,6},{9,8},{11,10},{13,12},{15,14},{17,16},{19,... | collective-permute-start | bytes 196616 | tf_op jit(solution)/shard_map/ppermute | solution.py:15
  100.0 14.5 %collective-permute-start.6 = (bf16[1,64,4,1,128]{1,3,4,2,0:T(2,128)(2,1)S(1)}, bf16[1,64,4,1,128]{1,3,4,2,0:T(2,128)(2,1)S(1)}, u32[]{:S(2)}, u32[]{:S(2)}) collective-permute-start(bf16[1,64,4,1,128]{1,3,4,2,0:T(2,128)(2,1)S(1)} %get-tuple-element.22), channel_id=1, source_target_pairs={{0,1},{2,3},{4,5},{6,7},{8,9},{10,11},{12,13},{14,15},{16,17},{18,... | collective-permute-start | bytes 196616 | tf_op jit(solution)/shard_map/ppermute | solution.py:14
  117.3 0.7 copy-start.9
Sparse Core Ops, SparseCore 0:
  74.5 39.9 all-reduce.2
  122.3 55.6 all-reduce.4
